TPU v7x, 32 devices: a whole 2x2x4 slice. The times are simulated.
32 devices in a mesh: dp: 4 (over y, core), expert: 8 (over z, x).
Axes of the slice: x: 2, y: 2, z: 4, core: 2. Of those that a mesh axis runs over, the one named last changes fastest.
Arguments:
- hidden_in: bfloat16 [2048, 2048], P(('dp', 'expert')), may hold values from -6 to 6
- context: bfloat16 [2048, 2048], P(('dp', 'expert')), may hold values from -6 to 6
- out_proj: bfloat16 [2048, 2048], P(('dp', 'expert')), may hold values from -0.125 to 0.125
- norm_gain: float32 [2048], replicated, may hold values from 0.5 to 1.5
- router: bfloat16 [2048, 64], P(('dp', 'expert')), may hold values from -0.25 to 0.25
- expert_ids: int32 [2048, 8], P(('dp', 'expert')), may hold values from 0 to 63, as said below
- replica_expert: int32 [128], replicated, may hold values from 0 to 63, as said below
- split_pick: int32 [2048, 8], P(('dp', 'expert')), may hold values from 0 to 65535
- up_gate: bfloat16 [128, 2048, 2048], P(('dp', 'expert')), may hold values from -0.125 to 0.125
- down: bfloat16 [128, 1024, 2048], P(('dp', 'expert')), may hold values from -0.1875 to 0.1875
Outputs:
- layer_out: bfloat16 [2048, 2048], P(('dp', 'expert'))
Inputs may be any that keep to these rules, and one draw needn't show every extreme that they name: `expert_ids`: each row names 8 different experts. `replica_expert`: every expert is served by one replica or more.
All inputs are finite; a program needn't handle non-finite values.
Results may differ from a plain program's by a relative error of at most 0.004.
Values may be sent and summed in bfloat16 or wider, within the bound.
A program may use at most 128 MiB of HBM per device.

v0:
```python
import jax
import jax.numpy as jnp
from jax import lax
from jax.sharding import PartitionSpec as P


def rms_norm(residual, norm_gain):
    scale_back = lax.rsqrt(jnp.mean(residual * residual, axis=-1, keepdims=True) + 1e-05)
    return (residual * scale_back * norm_gain).astype(jnp.bfloat16)


def route_block(expert_ids, split_pick, replica_expert):
    replica_total = replica_expert.shape[0]
    replica_iota = lax.iota(jnp.int32, replica_total)
    same_expert = replica_expert[:, None] == replica_expert[None, :]
    earlier = replica_iota[:, None] > replica_iota[None, :]
    replica_rank = jnp.sum((same_expert & earlier).astype(jnp.int32), axis=1)
    serves = expert_ids[:, :, None] == replica_expert[None, None, :]
    replica_count = jnp.sum(serves.astype(jnp.int32), axis=-1)
    wanted = split_pick % replica_count
    matches = serves & (replica_rank[None, None, :] == wanted[:, :, None])
    replica = jnp.sum(jnp.where(matches, replica_iota[None, None, :], 0), axis=-1)
    flat_replica = replica.reshape(-1)
    pair_iota = lax.iota(jnp.int32, flat_replica.shape[0])
    same_target = flat_replica[:, None] == flat_replica[None, :]
    before = pair_iota[:, None] > pair_iota[None, :]
    slot_index = jnp.sum((same_target & before).astype(jnp.int32), axis=1)
    return (replica, slot_index.reshape(replica.shape))


def apply_experts(incoming, up_gate, down, capacity):
    arrived_shape = incoming.shape
    local_reps = up_gate.shape[0]
    hidden_units = down.shape[1]
    stacked = incoming.reshape(-1, local_reps, capacity, incoming.shape[-1])
    gate_up = jnp.einsum("sjcd,jdf->sjcf", stacked, up_gate, preferred_element_type=jnp.float32)
    hidden_act = (jax.nn.silu(gate_up[..., :hidden_units]) * gate_up[..., hidden_units:]).astype(
        jnp.bfloat16
    )
    expert_out = jnp.einsum("sjcf,jfd->sjcd", hidden_act, down, preferred_element_type=jnp.float32)
    return expert_out.astype(jnp.bfloat16).reshape(arrived_shape)


def per_device(
    hidden_in,
    context,
    out_proj,
    norm_gain,
    router,
    expert_ids,
    replica_expert,
    split_pick,
    up_gate,
    down,
):
    tok_rows, model_width = hidden_in.shape
    top_count = expert_ids.shape[1]
    replica_total = replica_expert.shape[0]
    local_reps = up_gate.shape[0]
    data_groups = lax.axis_size("dp")
    expert_groups = lax.axis_size("expert")
    capacity = max(2, 2 * tok_rows * top_count // replica_total)
    summed = jnp.dot(
        context,
        lax.all_gather(out_proj, ("dp", "expert"), axis=0, tiled=True),
        preferred_element_type=jnp.float32,
    )
    router_rows = lax.all_gather(router, ("dp", "expert"), axis=0, tiled=True)
    residual = hidden_in.astype(jnp.float32) + summed
    normed = rms_norm(residual, norm_gain)
    logits = jnp.dot(normed, router_rows, preferred_element_type=jnp.float32)
    hit_mask = expert_ids[:, :, None] == lax.iota(jnp.int32, logits.shape[1])[None, None, :]
    chosen = jnp.sum(jnp.where(hit_mask, logits[:, None, :], 0.0), axis=-1)
    raised = jnp.exp(chosen)
    route_weight = raised / jnp.sum(raised, axis=-1, keepdims=True)
    replica, slot_index = route_block(expert_ids, split_pick, replica_expert)
    within_cap = slot_index < capacity
    buffer_row = jnp.where(within_cap, replica * capacity + slot_index, -1).reshape(-1)
    slot_total = replica_total * capacity
    matches = buffer_row[None, :] == lax.iota(jnp.int32, slot_total)[:, None]
    filled = jnp.any(matches, axis=1)
    row_of_pair = lax.iota(jnp.int32, tok_rows * top_count) // top_count
    anchor = jnp.sum(jnp.where(matches, row_of_pair[None, :], 0), axis=1)
    outgoing = jnp.where(filled[:, None], normed[anchor], jnp.zeros((), jnp.bfloat16))
    outgoing = outgoing.reshape(data_groups, expert_groups, local_reps * capacity, model_width)
    incoming = lax.all_to_all(
        lax.all_to_all(outgoing, "expert", split_axis=1, concat_axis=1, tiled=True),
        "dp",
        split_axis=0,
        concat_axis=0,
        tiled=True,
    )
    results = apply_experts(incoming, up_gate, down, capacity)
    returned = lax.all_to_all(
        lax.all_to_all(results, "dp", split_axis=0, concat_axis=0, tiled=True),
        "expert",
        split_axis=1,
        concat_axis=1,
        tiled=True,
    )
    returned = returned.reshape(slot_total, model_width)
    safe_index = jnp.where(within_cap, replica * capacity + slot_index, 0)
    gathered = returned[safe_index]
    kept_weight = jnp.where(within_cap, route_weight, 0.0)
    layer_out = residual + jnp.sum(kept_weight[:, :, None] * gathered.astype(jnp.float32), axis=1)
    return layer_out.astype(jnp.bfloat16)


def solution(mesh):
    return jax.shard_map(
        per_device,
        mesh=mesh,
        in_specs=(
            P(("dp", "expert"), None),
            P(("dp", "expert"), None),
            P(("dp", "expert"), None),
            P(),
            P(("dp", "expert"), None),
            P(("dp", "expert"), None),
            P(),
            P(("dp", "expert"), None),
            P(("dp", "expert"), None, None),
            P(("dp", "expert"), None, None),
        ),
        out_specs=P(("dp", "expert"), None),
        check_vma=False,
    )
```

profile of v0, /device:TPU:0, one launch (start us, length us, event | category | flops | bytes accessed | tf_op | source)
XLA Modules:
  0.0 520.4 jit_solution(7582275169445691453)
XLA Ops:
  6.5 0.0 copy-start
  6.5 0.0 all-gather.2.cloned.1.call-start
  6.5 0.7 all-gather.2.cloned.1.call-update
  7.3 0.8 copy.38
  8.0 0.8 copy.39
  8.8 0.9 convert_reduce_fusion.1
  9.7 1.9 fusion.16
  11.6 0.4 add_select_fusion
  12.0 2.0 select_reduce_fusion.2
  13.9 0.1 eq.94
  14.0 0.3 convert_reduce_fusion
  14.3 0.3 fusion.14
  14.6 0.1 broadcast_in_dim.93
  14.7 0.3 select_reduce_fusion
  15.0 0.0 copy-start.3
  15.0 75.5 %all-gather.2.cloned.1.call-done = bf16[2048,2048]{1,0:T(8,128)(2,1)} async-done(((bf16[64,2048]{1,0:T(8,128)(2,1)}), bf16[2048,2048]{1,0:T(8,128)(2,1)}) %all-gather.2.cloned.1.call-update) | async-done | bytes 8388624 | tf_op jit(solution)/shard_map/all_gather | solution.py:65
  90.5 0.0 copy-done
  90.5 5.1 multiply_reduce_fusion
  95.6 0.0 copy-done.3
  95.6 0.1 multiply_convert_fusion
  95.7 6.0 %gather_fusion = bf16[1024,2048]{1,0:T(8,128)(2,1)} fusion(bf16[64,2048]{1,0:T(8,128)(2,1)S(1)} %multiply_convert_fusion, s32[1024]{0:T(1024)S(1)} %broadcast_clamp_fusion), kind=kCustom, calls=%fused_computation | custom fusion | bytes 8392704 | tf_op jit(solution)/shard_map/gather | solution.py:84
  101.7 2.5 copy_select_fusion
  104.2 97.4 %all_to_all.20 = bf16[4,8,32,2048]{3,2,0,1:T(8,128)(2,1)S(1)} all-to-all(bf16[4,8,32,2048]{3,2,0,1:T(8,128)(2,1)S(1)} %copy_select_fusion), channel_id=1, replica_groups=mesh['dp'=4,'expert'=8] {'expert'}, dimensions={1} | all-to-all | bytes 8388608 | tf_op jit(solution)/shard_map/all_to_all | solution.py:87
  201.6 0.6 copy.43
  202.2 51.7 %all_to_all.21 = bf16[4,8,32,2048]{3,2,1,0:T(8,128)(2,1)} all-to-all(bf16[4,8,32,2048]{3,2,1,0:T(8,128)(2,1)S(1)} %copy.43), channel_id=1, replica_groups=mesh['dp'=4,'expert'=8] {'dp'}, dimensions={0} | all-to-all | bytes 8388608 | tf_op jit(solution)/shard_map/all_to_all | solution.py:86
  253.9 18.3 %fusion.4 = f32[32,4,8,2048]{3,2,0,1:T(8,128)} fusion(bf16[4,2048,2048]{2,1,0:T(8,128)(2,1)} %param.18, bf16[32,4,8,2048]{3,2,1,0:T(8,128)(2,1)} %bitcast.39), kind=kOutput, calls=%fused_computation.6 | convolution fusion | flops 8589934592 | bytes 46137344 | tf_op jit(solution)/shard_map/sjcd,jdf->sjcf/dot_general | solution.py:36
  272.1 14.8 %convert_bitcast_fusion = bf16[32,4,8,2048]{3,2,0,1:T(8,128)(2,1)} fusion(bf16[4,1024,2048]{2,1,0:T(8,128)(2,1)} %param.19, f32[32,4,8,2048]{3,2,0,1:T(8,128)} %fusion.4), kind=kOutput, calls=%fused_computation.13 | convolution fusion | flops 4303355904 | bytes 29360128 | tf_op jit(solution)/shard_map/sjcf,jfd->sjcd/dot_general | solution.py:40
  287.0 2.5 copy.45
  289.5 50.7 %all_to_all.22 = bf16[4,8,32,2048]{3,2,1,0:T(8,128)(2,1)S(1)} all-to-all(bf16[4,8,32,2048]{3,2,1,0:T(8,128)(2,1)S(1)} %bitcast.42), channel_id=1, replica_groups=mesh['dp'=4,'expert'=8] {'dp'}, dimensions={0} | all-to-all | bytes 8388608 | tf_op jit(solution)/shard_map/all_to_all | solution.py:95
  340.2 2.3 copy.46
  342.5 0.0 copy-start.2
  342.5 4.7 all-to-all-start.3
  347.2 0.1 reshape.142
  347.3 0.1 lt.57
  347.4 0.1 reshape.153
  347.5 0.0 copy-done.2
  347.5 150.8 %all_gather.7 = bf16[2048,64]{1,0:T(8,128)(2,1)S(1)} all-gather(bf16[64,64]{1,0:T(8,128)(2,1)S(1)} %copy-done.2), channel_id=1, replica_groups=mesh['dp'=4,'expert'=8] {'dp','expert'}, dimensions={0}, use_global_device_ids=true | all-gather | bytes 270336 | tf_op jit(solution)/shard_map/all_gather | solution.py:68
  498.3 0.2 fusion.23
  498.6 0.2 select_reduce_fusion.1
  498.8 0.1 exponential_reduce_fusion
  498.9 0.1 divide_select_fusion
  499.0 0.0 all-to-all-done.3
  499.0 4.7 copy.47
  503.8 0.0 copy-start.1
  503.8 7.2 %gather_fusion.1 = bf16[512,2048]{1,0:T(8,128)(2,1)S(1)} fusion(bf16[1024,2048]{1,0:T(8,128)(2,1)} %bitcast.40, s32[1024]{0:T(1024)S(1)} %pad_clamp_fusion), kind=kCustom, calls=%fused_computation.1 | custom fusion | bytes 4196352 | tf_op jit(solution)/shard_map/gather | solution.py:103
  511.0 1.8 fusion.8
  512.8 0.8 add_convert_fusion
  513.6 0.0 copy-done.1
  (8 shorter events, 0.1 us)
Async XLA Ops:
  6.5 84.0 %copy-start = (bf16[64,2048]{1,0:T(8,128)(2,1)S(1)}, bf16[64,2048]{1,0:T(8,128)(2,1)}, u32[]{:S(2)}) copy-start(bf16[64,2048]{1,0:T(8,128)(2,1)} %param.11) | copy-start | bytes 786436
  6.5 84.0 %all-gather.2.cloned.1.call-start = ((), (), s32[]{:S(2)}) async-start(), calls=%async_computation.4 | async-start | bytes 8650752 | tf_op jit(solution)/shard_map/all_gather | solution.py:65
  15.0 80.6 %copy-start.3 = (f32[2048]{0:T(1024)S(1)}, f32[2048]{0:T(1024)}, u32[]{:S(2)}) copy-start(f32[2048]{0:T(1024)} %param.13) | copy-start | bytes 24580
  342.5 5.0 copy-start.2
  342.5 156.5 %all-to-all-start.3 = ((bf16[4,8,32,2048]{3,2,0,1:T(8,128)(2,1)}), bf16[4,8,32,2048]{3,2,0,1:T(8,128)(2,1)}, u32[]{:S(2)}, u32[]{:S(2)}) async-start(bf16[4,8,32,2048]{3,2,0,1:T(8,128)(2,1)} %copy.46), calls=%async_computation.3 | async-start | bytes 8388608 | tf_op jit(solution)/shard_map/all_to_all | solution.py:94
  503.8 9.8 %copy-start.1 = (bf16[64,2048]{1,0:T(8,128)(2,1)S(1)}, bf16[64,2048]{1,0:T(8,128)(2,1)}, u32[]{:S(2)}) copy-start(bf16[64,2048]{1,0:T(8,128)(2,1)} %param.11) | copy-start | bytes 786436
Sparse Core Ops, SparseCore 0:
  10.3 80.1 all-gather.1
where the time goes:
time: 521 us; the launch traced here: 520 us
  blocking collectives  351 us (67%)
  waiting for transfers between devices  76.2 us (15%)
  matrix products  38.4 us (7%)
  local copies, waits for them, and re-layouts  25.3 us (5%)
  between operations  13.6 us (3%)
  other arithmetic  11.6 us (2%)
    all_gather x1, blocking collectives, per_device(): router_rows = lax.all_gather(router, ('dp', 'expert'), axis=0, tiled=True)  151 us
    all_to_all x1, blocking collectives, per_device(): lax.all_to_all(outgoing, 'expert', split_axis=1, concat_axis=1, tiled=True)  97.4 us
    all_gather x1, waiting for transfers between devices, per_device(): lax.all_gather(out_proj, ('dp', 'expert'), axis=0, tiled=True)  75.5 us
    all_to_all x1, blocking collectives, per_device(): lax.all_to_all(lax.all_to_all(outgoing, 'expert', split_axis=1, concat_ax...  51.7 us
    all_to_all x1, blocking collectives, per_device(): lax.all_to_all(results, 'dp', split_axis=0, concat_axis=0, tiled=True)  50.7 us
    dot_general x1, matrix products, apply_experts(): jnp.einsum('sjcd,jdf->sjcf', stacked, up_gate, preferred_element_type=jnp...  18.3 us
    dot_general x1, matrix products, apply_experts(): jnp.einsum('sjcf,jfd->sjcd', hidden_act, down, preferred_element_type=jnp...  14.8 us
  transfers between devices with their start and end apart: 2, of which 1 were waited for; matrix products, arithmetic and copies ran while one was open for 2% of the time, Pallas kernels for 0%

commit v1 on v0

--- a/solution.py
+++ b/solution.py
@@ -2,6 +2,17 @@
 import jax.numpy as jnp
 from jax import lax
 from jax.sharding import PartitionSpec as P
+
+
+def in_blocks(shard, dim, size):
+    before, after = (shard.shape[:dim], shard.shape[dim + 1 :])
+    return jnp.moveaxis(shard.reshape(*before, size, -1, *after), dim, 0)
+
+
+def in_order(blocks, dim):
+    blocks = jnp.moveaxis(blocks, 0, dim)
+    dims = blocks.shape
+    return blocks.reshape(*dims[:dim], dims[dim] * dims[dim + 1], *dims[dim + 2 :])
 
 
 def rms_norm(residual, norm_gain):
@@ -91,13 +102,15 @@
         tiled=True,
     )
     results = apply_experts(incoming, up_gate, down, capacity)
-    returned = lax.all_to_all(
-        lax.all_to_all(results, "dp", split_axis=0, concat_axis=0, tiled=True),
-        "expert",
-        split_axis=1,
-        concat_axis=1,
-        tiled=True,
-    )
+    shard = lax.all_to_all(results, "dp", split_axis=0, concat_axis=0, tiled=True)
+    size, mine = (lax.axis_size("expert"), lax.axis_index("expert"))
+    blocks = in_blocks(shard, 1, size)
+    outs = [blocks[mine]]
+    for step in range(1, size):
+        sent = blocks[(mine + step) % size]
+        outs.append(lax.ppermute(sent, "expert", [(i, (i + step) % size) for i in range(size)]))
+    blocks = jnp.stack(outs)[(mine - jnp.arange(size)) % size]
+    returned = in_order(blocks, 1)
     returned = returned.reshape(slot_total, model_width)
     safe_index = jnp.where(within_cap, replica * capacity + slot_index, 0)
     gathered = returned[safe_index]

time: 521 us -> 490 us (0.940)
  blocking collectives: 351 us -> 220 us
  waiting for transfers between devices: 76.2 us -> 141 us
  starting transfers between devices: 4.68 us -> 21.7 us
  local copies, waits for them, and re-layouts: 25.3 us -> 40.5 us
    all_gather x1, blocking collectives: 151 us -> 70.8 us  [per_device(): router_rows = lax.all_gather(router, ('dp', 'expert'), axis=0, tiled=True)]
    ppermute x0 -> x7, waiting for transfers between devices: none -> 64.5 us  [per_device(): lax.ppermute(sent, 'expert', [(i, (i + step) % size) for i in range(size)])]
    all_to_all x1 -> x0, blocking collectives: 50.7 us -> none  [per_device(): lax.all_to_all(results, 'dp', split_axis=0, concat_axis=0, tiled=True)]
    ppermute x0 -> x7, starting transfers between devices: none -> 16.7 us  [per_device(): lax.ppermute(sent, 'expert', [(i, (i + step) % size) for i in range(size)])]
    unnamed x10 -> x18, local copies, waits for them, and re-layouts: 1.56 us -> 11 us
    all_to_all x2 -> x0, local copies, waits for them, and re-layouts: 7.02 us -> none  [the longest x1 4.75 us: per_device(): lax.all_to_all(lax.all_to_all(results, 'dp', split_axis=0, concat_axis=0,...]
  transfers between devices with their start and end apart: 2 -> 9, of which waited for: 1 -> 5; matrix products, arithmetic and copies ran while one was open for 2% -> 3% of each run, Pallas kernels for 0% -> 0%
where the time goes in v1:
time: 490 us; the launch traced here: 486 us
  blocking collectives  220 us (45%)
  waiting for transfers between devices  141 us (29%)
  local copies, waits for them, and re-layouts  40.5 us (8%)
  matrix products  38.4 us (8%)
  starting transfers between devices  21.7 us (4%)
  between operations  13.8 us (3%)
  other arithmetic  11.7 us (2%)
    all_to_all x1, blocking collectives, per_device(): lax.all_to_all(outgoing, 'expert', split_axis=1, concat_axis=1, tiled=True)  97.4 us
    all_gather x1, waiting for transfers between devices, per_device(): lax.all_gather(out_proj, ('dp', 'expert'), axis=0, tiled=True)  75.5 us
    all_gather x1, blocking collectives, per_device(): router_rows = lax.all_gather(router, ('dp', 'expert'), axis=0, tiled=True)  70.8 us
    ppermute x7, waiting for transfers between devices, per_device(): lax.ppermute(sent, 'expert', [(i, (i + step) % size) for i in range(size)])  64.5 us
    all_to_all x1, blocking collectives, per_device(): lax.all_to_all(lax.all_to_all(outgoing, 'expert', split_axis=1, concat_ax...  51.7 us
    dot_general x1, matrix products, apply_experts(): jnp.einsum('sjcd,jdf->sjcf', stacked, up_gate, preferred_element_type=jnp...  18.3 us
    ppermute x7, starting transfers between devices, per_device(): lax.ppermute(sent, 'expert', [(i, (i + step) % size) for i in range(size)])  16.7 us
    dot_general x1, matrix products, apply_experts(): jnp.einsum('sjcf,jfd->sjcd', hidden_act, down, preferred_element_type=jnp...  14.8 us
  transfers between devices with their start and end apart: 9, of which 5 were waited for; matrix products, arithmetic and copies ran while one was open for 3% of the time, Pallas kernels for 0%

profile of v1, /device:TPU:0, one launch (start us, length us, event | category | flops | bytes accessed | tf_op | source)
XLA Modules:
  0.0 486.4 jit_solution(17880633017927560534)
XLA Ops:
  6.5 0.7 all-gather.2.cloned.1.call-update
  7.3 0.8 copy.76
  8.0 0.8 copy.77
  8.8 0.9 convert_reduce_fusion.1
  9.7 1.9 fusion.16
  11.6 0.4 add_select_fusion
  12.0 2.0 select_reduce_fusion.2
  14.0 0.3 convert_reduce_fusion
  14.3 0.3 fusion.14
  14.7 0.3 select_reduce_fusion
  15.0 75.5 %all-gather.2.cloned.1.call-done = bf16[2048,2048]{1,0:T(8,128)(2,1)} async-done(((bf16[64,2048]{1,0:T(8,128)(2,1)}), bf16[2048,2048]{1,0:T(8,128)(2,1)}) %all-gather.2.cloned.1.call-update) | async-done | bytes 8388624 | tf_op jit(solution)/shard_map/all_gather | solution.py:76
  90.5 5.1 %multiply_reduce_fusion = (f32[64]{0:T(128)S(1)}, f32[64,2048]{1,0:T(8,128)S(1)}) fusion(bf16[64,2048]{1,0:T(8,128)(2,1)S(1)} %copy-done, bf16[2048,2048]{1,0:T(8,128)(2,1)} %all-gather.2.cloned.1.call-done, bf16[64,2048]{1,0:T(8,128)(2,1)} %param.10), kind=kOutput, calls=%fused_computation.40 | convolution fusion | flops 537395136 | bytes 9437440 | tf_op jit(solution)/shard_map/dot_general | solution.py:74
  95.6 0.1 multiply_convert_fusion
  95.7 6.0 %gather_fusion = bf16[1024,2048]{1,0:T(8,128)(2,1)} fusion(bf16[64,2048]{1,0:T(8,128)(2,1)S(1)} %multiply_convert_fusion, s32[1024]{0:T(1024)S(1)} %broadcast_clamp_fusion), kind=kCustom, calls=%fused_computation | custom fusion | bytes 8392704 | tf_op jit(solution)/shard_map/gather | solution.py:95
  101.7 2.5 copy_select_fusion
  104.2 97.4 %all_to_all.15 = bf16[4,8,32,2048]{3,2,0,1:T(8,128)(2,1)S(1)} all-to-all(bf16[4,8,32,2048]{3,2,0,1:T(8,128)(2,1)S(1)} %copy_select_fusion), channel_id=1, replica_groups=mesh['dp'=4,'expert'=8] {'expert'}, dimensions={1} | all-to-all | bytes 8388608 | tf_op jit(solution)/shard_map/all_to_all | solution.py:98
  201.6 0.6 copy.81
  202.2 51.7 %all_to_all.16 = bf16[4,8,32,2048]{3,2,1,0:T(8,128)(2,1)} all-to-all(bf16[4,8,32,2048]{3,2,1,0:T(8,128)(2,1)S(1)} %copy.81), channel_id=1, replica_groups=mesh['dp'=4,'expert'=8] {'dp'}, dimensions={0} | all-to-all | bytes 8388608 | tf_op jit(solution)/shard_map/all_to_all | solution.py:97
  253.9 18.3 %fusion.4 = f32[32,4,8,2048]{3,2,0,1:T(8,128)} fusion(bf16[4,2048,2048]{2,1,0:T(8,128)(2,1)} %param.18, bf16[32,4,8,2048]{3,2,1,0:T(8,128)(2,1)} %bitcast.75), kind=kOutput, calls=%fused_computation.7 | convolution fusion | flops 8589934592 | bytes 46137344 | tf_op jit(solution)/shard_map/sjcd,jdf->sjcf/dot_general | solution.py:47
  272.1 14.8 %convert_bitcast_fusion = bf16[32,4,8,2048]{3,2,0,1:T(8,128)(2,1)} fusion(bf16[4,1024,2048]{2,1,0:T(8,128)(2,1)} %param.19, f32[32,4,8,2048]{3,2,0,1:T(8,128)} %fusion.4), kind=kOutput, calls=%fused_computation.14 | convolution fusion | flops 4303355904 | bytes 29360128 | tf_op jit(solution)/shard_map/sjcf,jfd->sjcd/dot_general | solution.py:51
  287.0 4.7 copy.83
  291.7 5.0 %all-to-all-start.2 = ((bf16[4,8,32,2048]{3,2,1,0:T(8,128)(2,1)}), bf16[4,8,32,2048]{3,2,1,0:T(8,128)(2,1)}, u32[]{:S(2)}, u32[]{:S(2)}) async-start(bf16[4,8,32,2048]{3,2,1,0:T(8,128)(2,1)} %bitcast.78), calls=%async_computation.2 | async-start | bytes 8388608 | tf_op jit(solution)/shard_map/all_to_all | solution.py:105
  297.2 70.8 %all_gather.7 = bf16[2048,64]{1,0:T(8,128)(2,1)S(1)} all-gather(bf16[64,64]{1,0:T(8,128)(2,1)S(1)} %copy-done.2), channel_id=1, replica_groups=mesh['dp'=4,'expert'=8] {'dp','expert'}, dimensions={0}, use_global_device_ids=true | all-gather | bytes 270336 | tf_op jit(solution)/shard_map/all_gather | solution.py:79
  368.0 0.2 fusion.25
  368.2 0.2 select_reduce_fusion.1
  368.4 2.5 dynamic-slice_bitcast_fusion
  370.9 3.9 collective-permute-start
  375.0 1.0 collective-permute-start.6
  376.0 2.0 collective-permute-start.1
  378.0 1.9 bitcast_dynamic-update-slice_fusion.7
  379.9 11.6 %collective-permute-done = bf16[4,1,32,2048]{3,2,0,1:T(8,128)(2,1)S(1)} collective-permute-done((bf16[4,1,32,2048]{3,2,0,1:T(8,128)(2,1)S(1)}, bf16[4,1,32,2048]{3,2,0,1:T(8,128)(2,1)S(1)}, u32[]{:S(2)}, u32[]{:S(2)}) %collective-permute-start) | collective-permute-done | bytes 524320 | tf_op jit(solution)/shard_map/ppermute | solution.py:111
  391.4 0.8 collective-permute-start.2
  392.3 0.9 bitcast_dynamic-update-slice_fusion.6
  393.1 27.7 %collective-permute-done.1 = bf16[4,1,32,2048]{3,2,0,1:T(8,128)(2,1)S(1)} collective-permute-done((bf16[4,1,32,2048]{3,2,0,1:T(8,128)(2,1)S(1)}, bf16[4,1,32,2048]{3,2,0,1:T(8,128)(2,1)S(1)}, u32[]{:S(2)}, u32[]{:S(2)}) %collective-permute-start.1) | collective-permute-done | bytes 524320 | tf_op jit(solution)/shard_map/ppermute | solution.py:111
  420.8 9.0 %collective-permute-start.3 = (bf16[4,1,32,2048]{3,2,0,1:T(8,128)(2,1)S(1)}, bf16[4,1,32,2048]{3,2,0,1:T(8,128)(2,1)S(1)}, u32[]{:S(2)}, u32[]{:S(2)}) collective-permute-start(bf16[4,1,32,2048]{3,2,0,1:T(8,128)(2,1)S(1)} %get-tuple-element.8), channel_id=1, source_target_pairs={{0,4},{1,5},{2,6},{3,7},{4,0},{5,1},{6,2},{7,3},{8,12},{9,13},{10,... | collective-permute-start | bytes 1572872 | tf_op jit(solution)/shard_map/ppermute | solution.py:111
  429.8 0.8 bitcast_dynamic-update-slice_fusion.5
  430.7 18.7 %collective-permute-done.2 = bf16[4,1,32,2048]{3,2,0,1:T(8,128)(2,1)S(1)} collective-permute-done((bf16[4,1,32,2048]{3,2,0,1:T(8,128)(2,1)S(1)}, bf16[4,1,32,2048]{3,2,0,1:T(8,128)(2,1)S(1)}, u32[]{:S(2)}, u32[]{:S(2)}) %collective-permute-start.2) | collective-permute-done | bytes 524320 | tf_op jit(solution)/shard_map/ppermute | solution.py:111
  449.4 0.8 bitcast_dynamic-update-slice_fusion.4
  450.2 6.5 %collective-permute-done.3 = bf16[4,1,32,2048]{3,2,0,1:T(8,128)(2,1)S(1)} collective-permute-done((bf16[4,1,32,2048]{3,2,0,1:T(8,128)(2,1)S(1)}, bf16[4,1,32,2048]{3,2,0,1:T(8,128)(2,1)S(1)}, u32[]{:S(2)}, u32[]{:S(2)}) %collective-permute-start.3) | collective-permute-done | bytes 524320 | tf_op jit(solution)/shard_map/ppermute | solution.py:111
  456.7 0.8 bitcast_dynamic-update-slice_fusion.3
  457.6 0.9 bitcast_dynamic-update-slice_fusion.2
  458.4 0.8 bitcast_dynamic-update-slice_fusion.1
  459.3 0.8 bitcast_dynamic-update-slice_fusion
  460.1 4.9 %gather_fusion.1 = bf16[8,4,32,2048]{3,2,1,0:T(8,128)(2,1)} fusion(bf16[8,4,32,2048]{3,2,1,0:T(8,128)(2,1)} %bitcast.19, s32[1024]{0:T(1024)S(1)} %pad_clamp_fusion.1), kind=kCustom, calls=%fused_computation.1 | custom fusion | bytes 8388640 | tf_op jit(solution)/shard_map/gather | solution.py:112
  465.0 4.7 copy.91
  469.8 7.2 %gather_fusion.2 = bf16[512,2048]{1,0:T(8,128)(2,1)S(1)} fusion(bf16[1024,2048]{1,0:T(8,128)(2,1)} %bitcast.76, s32[1024]{0:T(1024)S(1)} %pad_clamp_fusion), kind=kCustom, calls=%fused_computation.2 | custom fusion | bytes 4196352 | tf_op jit(solution)/shard_map/gather | solution.py:116
  477.0 1.8 fusion.8
  478.8 0.8 add_convert_fusion
  (32 shorter events, 0.8 us)
Async XLA Ops:
  6.5 84.0 %copy-start = (bf16[64,2048]{1,0:T(8,128)(2,1)S(1)}, bf16[64,2048]{1,0:T(8,128)(2,1)}, u32[]{:S(2)}) copy-start(bf16[64,2048]{1,0:T(8,128)(2,1)} %param.11) | copy-start | bytes 786436
  6.5 84.0 %all-gather.2.cloned.1.call-start = ((), (), s32[]{:S(2)}) async-start(), calls=%async_computation.3 | async-start | bytes 8650752 | tf_op jit(solution)/shard_map/all_gather | solution.py:76
  15.0 80.6 %copy-start.3 = (f32[2048]{0:T(1024)S(1)}, f32[2048]{0:T(1024)}, u32[]{:S(2)}) copy-start(f32[2048]{0:T(1024)} %param.13) | copy-start | bytes 24580
  291.7 5.5 %copy-start.2 = (bf16[64,64]{1,0:T(8,128)(2,1)S(1)}, bf16[64,64]{1,0:T(8,128)(2,1)}, u32[]{:S(2)}) copy-start(bf16[64,64]{1,0:T(8,128)(2,1)} %param.14) | copy-start | bytes 24580
  291.7 76.7 %all-to-all-start.2 = ((bf16[4,8,32,2048]{3,2,1,0:T(8,128)(2,1)}), bf16[4,8,32,2048]{3,2,1,0:T(8,128)(2,1)}, u32[]{:S(2)}, u32[]{:S(2)}) async-start(bf16[4,8,32,2048]{3,2,1,0:T(8,128)(2,1)} %bitcast.78), calls=%async_computation.2 | async-start | bytes 8388608 | tf_op jit(solution)/shard_map/all_to_all | solution.py:105
  370.9 20.5 %collective-permute-start = (bf16[4,1,32,2048]{3,2,0,1:T(8,128)(2,1)S(1)}, bf16[4,1,32,2048]{3,2,0,1:T(8,128)(2,1)S(1)}, u32[]{:S(2)}, u32[]{:S(2)}) collective-permute-start(bf16[4,1,32,2048]{3,2,0,1:T(8,128)(2,1)S(1)} %get-tuple-element.11), channel_id=1, source_target_pairs={{0,1},{1,2},{2,3},{3,4},{4,5},{5,6},{6,7},{7,0},{8,9},{9,10},{10,1... | collective-permute-start | bytes 1572872 | tf_op jit(solution)/shard_map/ppermute | solution.py:111
  375.0 84.3 %collective-permute-start.6 = (bf16[4,1,32,2048]{3,2,0,1:T(8,128)(2,1)S(1)}, bf16[4,1,32,2048]{3,2,0,1:T(8,128)(2,1)S(1)}, u32[]{:S(2)}, u32[]{:S(2)}) collective-permute-start(bf16[4,1,32,2048]{3,2,0,1:T(8,128)(2,1)S(1)} %get-tuple-element.5), channel_id=1, source_target_pairs={{0,7},{1,0},{2,1},{3,2},{4,3},{5,4},{6,5},{7,6},{8,15},{9,8},{10,9... | collective-permute-start | bytes 1572872 | tf_op jit(solution)/shard_map/ppermute | solution.py:111
  375.9 82.5 %collective-permute-start.5 = (bf16[4,1,32,2048]{3,2,0,1:T(8,128)(2,1)S(1)}, bf16[4,1,32,2048]{3,2,0,1:T(8,128)(2,1)S(1)}, u32[]{:S(2)}, u32[]{:S(2)}) collective-permute-start(bf16[4,1,32,2048]{3,2,0,1:T(8,128)(2,1)S(1)} %get-tuple-element.6), channel_id=1, source_target_pairs={{0,6},{1,7},{2,0},{3,1},{4,2},{5,3},{6,4},{7,5},{8,14},{9,15},{10,... | collective-permute-start | bytes 1572872 | tf_op jit(solution)/shard_map/ppermute | solution.py:111
  375.9 81.6 %collective-permute-start.4 = (bf16[4,1,32,2048]{3,2,0,1:T(8,128)(2,1)S(1)}, bf16[4,1,32,2048]{3,2,0,1:T(8,128)(2,1)S(1)}, u32[]{:S(2)}, u32[]{:S(2)}) collective-permute-start(bf16[4,1,32,2048]{3,2,0,1:T(8,128)(2,1)S(1)} %get-tuple-element.7), channel_id=1, source_target_pairs={{0,5},{1,6},{2,7},{3,0},{4,1},{5,2},{6,3},{7,4},{8,13},{9,14},{10,... | collective-permute-start | bytes 1572872 | tf_op jit(solution)/shard_map/ppermute | solution.py:111
  376.0 44.8 %collective-permute-start.1 = (bf16[4,1,32,2048]{3,2,0,1:T(8,128)(2,1)S(1)}, bf16[4,1,32,2048]{3,2,0,1:T(8,128)(2,1)S(1)}, u32[]{:S(2)}, u32[]{:S(2)}) collective-permute-start(bf16[4,1,32,2048]{3,2,0,1:T(8,128)(2,1)S(1)} %get-tuple-element.10), channel_id=1, source_target_pairs={{0,2},{1,3},{2,4},{3,5},{4,6},{5,7},{6,0},{7,1},{8,10},{9,11},{10,... | collective-permute-start | bytes 1572872 | tf_op jit(solution)/shard_map/ppermute | solution.py:111
  391.4 57.9 %collective-permute-start.2 = (bf16[4,1,32,2048]{3,2,0,1:T(8,128)(2,1)S(1)}, bf16[4,1,32,2048]{3,2,0,1:T(8,128)(2,1)S(1)}, u32[]{:S(2)}, u32[]{:S(2)}) collective-permute-start(bf16[4,1,32,2048]{3,2,0,1:T(8,128)(2,1)S(1)} %get-tuple-element.9), channel_id=1, source_target_pairs={{0,3},{1,4},{2,5},{3,6},{4,7},{5,0},{6,1},{7,2},{8,11},{9,12},{10,... | collective-permute-start | bytes 1572872 | tf_op jit(solution)/shard_map/ppermute | solution.py:111
  420.8 35.9 %collective-permute-start.3 = (bf16[4,1,32,2048]{3,2,0,1:T(8,128)(2,1)S(1)}, bf16[4,1,32,2048]{3,2,0,1:T(8,128)(2,1)S(1)}, u32[]{:S(2)}, u32[]{:S(2)}) collective-permute-start(bf16[4,1,32,2048]{3,2,0,1:T(8,128)(2,1)S(1)} %get-tuple-element.8), channel_id=1, source_target_pairs={{0,4},{1,5},{2,6},{3,7},{4,0},{5,1},{6,2},{7,3},{8,12},{9,13},{10,... | collective-permute-start | bytes 1572872 | tf_op jit(solution)/shard_map/ppermute | solution.py:111
  469.8 9.8 %copy-start.1 = (bf16[64,2048]{1,0:T(8,128)(2,1)S(1)}, bf16[64,2048]{1,0:T(8,128)(2,1)}, u32[]{:S(2)}) copy-start(bf16[64,2048]{1,0:T(8,128)(2,1)} %param.11) | copy-start | bytes 786436
Sparse Core Ops, SparseCore 0:
  10.3 80.1 all-gather.1
